TPU v7x, 512 devices: a whole 4x4x16 slice. The times are simulated.
512 devices in a mesh: grp: 16 (over y, x), tile: 32 (over z, core).
Axes of the slice: x: 4, y: 4, z: 16, core: 2. Of those that a mesh axis runs over, the one named last changes fastest.
Arguments:
- jac_point: float32 [6, 2097152], P(None, ('grp', 'tile')), may hold values from -6 to 6
- jac_cam: float32 [18, 2097152], P(None, ('grp', 'tile')), may hold values from -3 to 3
- resid: float32 [2, 2097152], P(None, ('grp', 'tile')), may hold values from -6 to 6
- point_index: int32 [2097152], P(('grp', 'tile')), may hold values from 0 to 4095, as said below
- cam_index: int32 [2097152], P(('grp', 'tile')), may hold values from 0 to 12287, as said below
Outputs:
- point_step: float32 [3, 2097152], P(None, ('grp', 'tile'))
- camera_step: float32 [9, 196608], P(None, ('grp', 'tile'))
- point_resid: float32 [3, 2097152], P(None, ('grp', 'tile'))
- camera_resid: float32 [9, 196608], P(None, ('grp', 'tile'))
Inputs may be any that keep to these rules, and one draw needn't show every extreme that they name: `point_index`: index among the points of the observation's own device; every device names point 0 and point 4096 - 1. `cam_index`: block h of a device's observations (slots h * 256 to (h + 1) * 256 - 1) names cameras of group h by their index within the group; every block names camera 0 and camera 12288 - 1.
All inputs are finite; a program needn't handle non-finite values.
Results may differ from a plain program's by a relative error of at most 0.0002.
Values sent between devices are 32-bit elements; how exact they have to be, the bound alone decides.
A program may use at most 64 MiB of HBM per device.

v0:
```python
import jax
import jax.numpy as jnp
from jax import lax
from jax.sharding import PartitionSpec as P

P_DEV = 4096
CAM_DEV = 384
ITERS = 2
damping = 1.0


def segment_rows(data, ids, count):
    return jax.vmap(lambda row: jax.ops.segment_sum(row, ids, num_segments=count))(data)


def shards(jac_point, jac_cam, resid, point_index, cam_index):
    obs_dev = jac_point.shape[1]
    cam_grp = CAM_DEV * lax.axis_size("tile")
    jp = jac_point.reshape(2, 3, obs_dev)
    jc = jac_cam.reshape(2, 9, obs_dev)
    owned_index = lax.all_to_all(cam_index, "grp", split_axis=0, concat_axis=0, tiled=True)
    point_rhs = segment_rows(-jnp.sum(jp * resid[:, None], axis=0), point_index, P_DEV)
    point_diag = segment_rows(jnp.sum(jp * jp, axis=0), point_index, P_DEV)
    grad_terms, square_terms = (
        lax.all_to_all(
            -jnp.sum(jc * resid[:, None], axis=0), "grp", split_axis=1, concat_axis=1, tiled=True
        ),
        lax.all_to_all(jnp.sum(jc * jc, axis=0), "grp", split_axis=1, concat_axis=1, tiled=True),
    )
    group_terms = segment_rows(
        jnp.concatenate([grad_terms, square_terms], axis=0), owned_index, cam_grp
    )
    camera_both = lax.psum_scatter(group_terms, "tile", scatter_dimension=1, tiled=True)
    camera_rhs, camera_diag = (camera_both[:9], camera_both[9:])

    def inner(ap, ac, bp, bc):
        return jnp.sum(ap * bp) + jnp.sum(ac * bc)

    def norm_sum(rp, rc, zp, zc):
        return lax.psum(inner(rp, rc, zp, zc), ("grp", "tile"))

    point_pre = point_diag + damping
    camera_pre = camera_diag + damping
    point_x = jnp.zeros_like(point_rhs)
    camera_x = jnp.zeros_like(camera_rhs)
    point_r, camera_r = (point_rhs, camera_rhs)
    point_z, camera_z = (point_r / point_pre, camera_r / camera_pre)
    point_dir, camera_dir = (point_z, camera_z)
    norm_now = norm_sum(point_r, camera_r, point_z, camera_z)
    for step_number in range(ITERS):
        group_cams = lax.all_gather(camera_dir, "tile", axis=1, tiled=True)
        fetched = group_cams[:, owned_index]
        point_term = jnp.sum(jp * point_dir[:, point_index][None], axis=1)
        at_obs = lax.all_to_all(fetched, "grp", split_axis=1, concat_axis=1, tiled=True)
        error = point_term + jnp.sum(jc * at_obs[None], axis=1)
        column = lax.all_to_all(
            jnp.sum(jc * error[:, None], axis=0), "grp", split_axis=1, concat_axis=1, tiled=True
        )
        camera_out = lax.psum_scatter(
            segment_rows(column, owned_index, cam_grp), "tile", scatter_dimension=1, tiled=True
        )
        point_out = segment_rows(jnp.sum(jp * error[:, None], axis=0), point_index, P_DEV)
        point_q = point_out + damping * point_dir
        camera_q = camera_out + damping * camera_dir
        curve = lax.psum(inner(point_dir, camera_dir, point_q, camera_q), ("grp", "tile"))
        alpha = norm_now / curve
        point_x = point_x + alpha * point_dir
        camera_x = camera_x + alpha * camera_dir
        point_r = point_r - alpha * point_q
        camera_r = camera_r - alpha * camera_q
        if step_number + 1 < ITERS:
            point_z, camera_z = (point_r / point_pre, camera_r / camera_pre)
            norm_next = norm_sum(point_r, camera_r, point_z, camera_z)
            ratio = norm_next / norm_now
            point_dir = point_z + ratio * point_dir
            camera_dir = camera_z + ratio * camera_dir
            norm_now = norm_next
    return (point_x, camera_x, point_r, camera_r)


def solution(mesh):
    placed = (
        P(None, ("grp", "tile")),
        P(None, ("grp", "tile")),
        P(None, ("grp", "tile")),
        P(("grp", "tile")),
        P(("grp", "tile")),
    )
    return jax.shard_map(
        shards,
        mesh=mesh,
        in_specs=placed,
        out_specs=(
            P(None, ("grp", "tile")),
            P(None, ("grp", "tile")),
            P(None, ("grp", "tile")),
            P(None, ("grp", "tile")),
        ),
        check_vma=False,
    )
```

profile of v0, /device:TPU:1, one launch (start us, length us, event | category | flops | bytes accessed | tf_op | source)
XLA Modules:
  0.0 1094.1 jit_solution(12470036015440183946)
XLA Ops:
  10.1 7.6 all-to-all-start.1
  18.5 6.8 all-to-all-done.1
  25.3 3.5 all-to-all-start.2
  29.3 7.1 all-to-all-done.2
  36.4 3.5 all-to-all-start
  40.9 5.3 all-to-all-done
  46.3 25.4 %scatter_custom_fusion.2 = f32[18,12288]{0,1:T(8,128)} fusion(s32[4096]{0:T(1024)S(1)} %bitcast.80, f32[4096,18]{1,0:T(8,128)S(1)} %copy.50, f32[]{:T(128)} %constant.5.clone.1), kind=kCustom, calls=%fused_computation.15 | custom fusion | flops 73728 | bytes 884740 | tf_op jit(solution)/shard_map/vmap()/scatter-add | solution.py:13
  71.7 119.8 %reduce-scatter.4.cloned.1.call-done = f32[18,384]{0,1:T(8,128)} async-done(((f32[18,12288]{0,1:T(8,128)}), f32[18,384]{0,1:T(8,128)}) %reduce-scatter.4.cloned.1.call-update) | async-done | bytes 27664 | tf_op jit(solution)/shard_map/reduce_scatter | solution.py:33
  192.7 57.6 %all_gather.6 = f32[9,12288]{0,1:T(8,128)} all-gather(f32[9,384]{0,1:T(8,128)S(1)} %fusion.11), channel_id=1, replica_groups=mesh['grp'=16,'tile'=32] {'tile'}, dimensions={1}, use_global_device_ids=true | all-gather | bytes 456192 | tf_op jit(solution)/shard_map/all_gather | solution.py:51
  250.3 13.6 %gather_fusion.1 = f32[4096,9]{1,0:T(8,128)S(1)} fusion(f32[9,12288]{0,1:T(8,128)} %all_gather.6, s32[4096]{0:T(1024)S(1)} %broadcast_clamp_fusion), kind=kCustom, calls=%fused_computation.1 | custom fusion | bytes 311296 | tf_op jit(solution)/shard_map/gather | solution.py:52
  265.2 6.4 all-to-all-start.3
  272.3 23.8 %scatter_custom_fusion = f32[3,4096]{0,1:T(8,128)} fusion(s32[4096]{0:T(1024)S(1)} %copy-done.5, f32[4096,3]{1,0:T(8,128)S(1)} %copy.43, f32[]{:T(128)} %constant.5.clone.1), kind=kCustom, calls=%fused_computation.27 | custom fusion | flops 12288 | bytes 49156 | tf_op jit(solution)/shard_map/vmap()/scatter-add | solution.py:13
  296.8 23.7 %scatter_custom_fusion.1 = f32[3,4096]{0,1:T(8,128)} fusion(s32[4096]{0:T(1024)S(1)} %copy-done.5, f32[4096,3]{1,0:T(8,128)S(1)} %copy.44, f32[]{:T(128)} %constant.6.clone.1), kind=kCustom, calls=%fused_computation.25 | custom fusion | flops 12288 | bytes 49156 | tf_op jit(solution)/shard_map/vmap()/scatter-add | solution.py:13
  323.0 14.2 %gather_fusion = f32[4096,3]{1,0:T(8,128)} fusion(f32[3,4096]{0,1:T(8,128)S(1)} %div.21, s32[4096]{0:T(1024)S(1)} %fusion.12), kind=kCustom, calls=%fused_computation | custom fusion | bytes 114688 | tf_op jit(solution)/shard_map/gather | solution.py:53
  340.3 14.0 %all_to_all.72 = f32[9,16,256]{2,0,1:T(8,128)S(1)} all-to-all(f32[9,16,256]{2,0,1:T(8,128)S(1)} %copy.55), channel_id=1, replica_groups=mesh['grp'=16,'tile'=32] {'grp'}, dimensions={1} | all-to-all | bytes 294912 | tf_op jit(solution)/shard_map/all_to_all | solution.py:56
  356.5 25.7 %scatter_custom_fusion.4 = f32[9,12288]{0,1:T(8,128)} fusion(s32[4096]{0:T(1024)S(1)} %bitcast.82, f32[4096,9]{1,0:T(8,128)} %copy.57, f32[]{:T(128)} %constant.5.clone.1), kind=kCustom, calls=%fused_computation.13 | custom fusion | flops 36864 | bytes 442880 | tf_op jit(solution)/shard_map/vmap()/scatter-add | solution.py:13
  384.3 23.4 %scatter_fusion = f32[3,4096]{0,1:T(8,128)S(1)} fusion(f32[3,4096]{0,1:T(8,128)S(1)} %copy-done.2, s32[4096]{0:T(1024)S(1)} %copy-done.5, f32[4096,3]{1,0:T(8,128)} %copy.54), kind=kCustom, calls=%fused_computation.7 | custom fusion | flops 12288 | bytes 163840 | tf_op jit(solution)/shard_map/vmap()/scatter-add | solution.py:13
  407.8 3.5 multiply_reduce_fusion.2
  411.2 82.1 %reduce-scatter.6.cloned.1.call-done = f32[9,384]{0,1:T(8,128)} async-done(((f32[9,12288]{0,1:T(8,128)}), f32[9,384]{0,1:T(8,128)}) %reduce-scatter.6.cloned.1.call-update) | async-done | bytes 13840 | tf_op jit(solution)/shard_map/reduce_scatter | solution.py:59
  497.6 106.2 %all-reduce = (f32[]{:T(128)}, f32[]{:T(128)}) all-reduce(f32[]{:T(128)S(6)} %add.103, f32[]{:T(128)S(6)} %add.108), channel_id=1, replica_groups=mesh['grp'=16,'tile'=32] {'grp','tile'}, use_global_device_ids=true, to_apply=%region_10.0 | all-reduce | flops 2 | bytes 16 | tf_op jit(solution)/shard_map/psum | solution.py:40
  605.1 5.3 multiply_reduce_fusion.1
  612.4 98.4 %psum.30 = f32[]{:T(128)} all-reduce(f32[]{:T(128)S(6)} %add.109), channel_id=1, replica_groups=mesh['grp'=16,'tile'=32] {'grp','tile'}, use_global_device_ids=true, to_apply=%region_23.0 | all-reduce | flops 1 | bytes 8 | tf_op jit(solution)/shard_map/psum | solution.py:40
  712.3 53.8 %all_gather.7 = f32[9,12288]{0,1:T(8,128)} all-gather(f32[9,384]{0,1:T(8,128)S(1)} %multiply_add_fusion.3), channel_id=1, replica_groups=mesh['grp'=16,'tile'=32] {'tile'}, dimensions={1}, use_global_device_ids=true | all-gather | bytes 456192 | tf_op jit(solution)/shard_map/all_gather | solution.py:51
  766.2 17.0 %gather_fusion.3 = f32[4096,9]{1,0:T(8,128)} fusion(f32[9,12288]{0,1:T(8,128)} %all_gather.7, s32[4096]{0:T(1024)S(1)} %broadcast_clamp_fusion), kind=kCustom, calls=%fused_computation.3 | custom fusion | bytes 311296 | tf_op jit(solution)/shard_map/gather | solution.py:52
  786.1 4.2 all-to-all-start.5
  793.7 15.7 %gather_fusion.2 = f32[4096,3]{1,0:T(8,128)} fusion(f32[3,4096]{0,1:T(8,128)} %multiply_add_fusion.1, s32[4096]{0:T(1024)S(1)} %fusion.12), kind=kCustom, calls=%fused_computation.2 | custom fusion | bytes 114688 | tf_op jit(solution)/shard_map/gather | solution.py:53
  813.4 14.4 %all_to_all.73 = f32[9,16,256]{2,0,1:T(8,128)S(1)} all-to-all(f32[9,16,256]{2,0,1:T(8,128)S(1)} %copy.62), channel_id=1, replica_groups=mesh['grp'=16,'tile'=32] {'grp'}, dimensions={1} | all-to-all | bytes 294912 | tf_op jit(solution)/shard_map/all_to_all | solution.py:56
  830.0 25.7 %scatter_custom_fusion.6 = f32[9,12288]{0,1:T(8,128)} fusion(s32[4096]{0:T(1024)S(1)} %bitcast.83, f32[4096,9]{1,0:T(8,128)} %copy.64, f32[]{:T(128)} %constant.5.clone.1), kind=kCustom, calls=%fused_computation.11 | custom fusion | flops 36864 | bytes 442880 | tf_op jit(solution)/shard_map/vmap()/scatter-add | solution.py:13
  860.8 23.3 %scatter_fusion.1 = f32[3,4096]{0,1:T(8,128)} fusion(f32[3,4096]{0,1:T(8,128)} %copy.80, s32[4096]{0:T(1024)S(1)} %copy-done.5, f32[4096,3]{1,0:T(8,128)} %copy.61), kind=kCustom, calls=%fused_computation.9 | custom fusion | flops 12288 | bytes 163840 | tf_op jit(solution)/shard_map/vmap()/scatter-add | solution.py:13
  887.4 78.7 %reduce-scatter.8.cloned.1.call-done = f32[9,384]{0,1:T(8,128)} async-done(((f32[9,12288]{0,1:T(8,128)}), f32[9,384]{0,1:T(8,128)}) %reduce-scatter.8.cloned.1.call-update) | async-done | bytes 13840 | tf_op jit(solution)/shard_map/reduce_scatter | solution.py:59
  969.0 106.2 %psum.31 = f32[]{:T(128)} all-reduce(f32[]{:T(128)S(6)} %add.114), channel_id=1, replica_groups=mesh['grp'=16,'tile'=32] {'grp','tile'}, use_global_device_ids=true, to_apply=%region_33.0 | all-reduce | flops 1 | bytes 8 | tf_op jit(solution)/shard_map/psum | solution.py:65
  1078.1 5.3 multiply_subtract_fusion
  (99 shorter events, 49.7 us)
Async XLA Ops:
  9.1 19.8 %copy-start.7 = (f32[6,4096]{1,0:T(8,128)S(1)}, f32[6,4096]{1,0:T(8,128)}, u32[]{:S(2)}) copy-start(f32[6,4096]{1,0:T(8,128)} %param.5) | copy-start | bytes 294916
  9.1 19.8 %copy-start.6 = (f32[2,4096]{1,0:T(2,128)S(1)}, f32[2,4096]{1,0:T(2,128)}, u32[]{:S(2)}) copy-start(f32[2,4096]{1,0:T(2,128)} %param.7) | copy-start | bytes 98308
  10.1 15.3 %all-to-all-start.1 = ((f32[9,16,256]{2,0,1:T(8,128)}), f32[9,16,256]{2,0,1:T(8,128)S(1)}, u32[]{:S(2)}, u32[]{:S(2)}) async-start(f32[9,16,256]{2,0,1:T(8,128)} %copy.46), calls=%async_computation.1 | async-start | bytes 524288 | tf_op jit(solution)/shard_map/all_to_all | solution.py:25
  25.3 11.0 %all-to-all-start.2 = ((f32[9,16,256]{2,0,1:T(8,128)}), f32[9,16,256]{2,0,1:T(8,128)S(1)}, u32[]{:S(2)}, u32[]{:S(2)}) async-start(f32[9,16,256]{2,0,1:T(8,128)} %copy.48), calls=%async_computation.2 | async-start | bytes 524288 | tf_op jit(solution)/shard_map/all_to_all | solution.py:28
  36.4 9.9 all-to-all-start
  39.9 151.6 %reduce-scatter.4.cloned.1.call-start = ((), (), s32[]{:S(2)}) async-start(), calls=%async_computation.10 | async-start | bytes 6488064 | tf_op jit(solution)/shard_map/reduce_scatter | solution.py:33
  250.2 21.4 %copy-start.5 = (s32[4096]{0:T(1024)S(1)}, s32[4096]{0:T(1024)}, u32[]{:S(2)}) copy-start(s32[4096]{0:T(1024)} %param.8) | copy-start | bytes 49156
  265.2 74.4 %all-to-all-start.3 = ((f32[9,16,256]{2,0,1:T(8,128)}), f32[9,16,256]{2,0,1:T(8,128)S(1)}, u32[]{:S(2)}, u32[]{:S(2)}) async-start(f32[9,16,256]{2,0,1:T(8,128)} %copy.52), calls=%async_computation.4 | async-start | bytes 524288 | tf_op jit(solution)/shard_map/all_to_all | solution.py:54
  271.6 221.7 %reduce-scatter.6.cloned.1.call-start = ((), (), s32[]{:S(2)}) async-start(), calls=%async_computation.11 | async-start | bytes 6488064 | tf_op jit(solution)/shard_map/reduce_scatter | solution.py:59
  323.0 59.2 %copy-start = (f32[3,4096]{0,1:T(8,128)}, f32[3,4096]{0,1:T(8,128)S(1)}, u32[]{:S(2)}) copy-start(f32[3,4096]{0,1:T(8,128)S(1)} %div.21) | copy-start | bytes 147460
  382.3 2.1 copy-start.2
  407.8 85.6 %copy-start.3 = (f32[18,384]{0,1:T(8,128)S(1)}, f32[18,384]{0,1:T(8,128)}, u32[]{:S(2)}) copy-start(f32[18,384]{0,1:T(8,128)} %reduce-scatter.4.cloned.1.call-done) | copy-start | bytes 82948
  766.2 24.4 %copy-start.1 = (f32[3,4096]{0,1:T(8,128)S(1)}, f32[3,4096]{0,1:T(8,128)}, u32[]{:S(2)}) copy-start(f32[3,4096]{0,1:T(8,128)} %copy-done) | copy-start | bytes 147460
  786.1 25.6 %all-to-all-start.5 = ((f32[9,16,256]{2,0,1:T(8,128)}), f32[9,16,256]{2,0,1:T(8,128)}, u32[]{:S(2)}, u32[]{:S(2)}) async-start(f32[9,16,256]{2,0,1:T(8,128)} %copy.59), calls=%async_computation.7 | async-start | bytes 524288 | tf_op jit(solution)/shard_map/all_to_all | solution.py:54
  790.3 175.8 %reduce-scatter.8.cloned.1.call-start = ((), (), s32[]{:S(2)}) async-start(), calls=%async_computation.12 | async-start | bytes 6488064 | tf_op jit(solution)/shard_map/reduce_scatter | solution.py:59
  1083.3 3.0 copy-start.4
Sparse Core Ops, SparseCore 0:
  71.8 119.6 reduce-scatter.3
  382.4 110.9 reduce-scatter.5
  855.8 110.2 reduce-scatter.7
where the time goes:
time: 1100 us; the launch traced here: 1090 us
  blocking collectives  451 us (41%)
  waiting for transfers between devices  300 us (27%)
  other arithmetic  201 us (18%)
  local copies, waits for them, and re-layouts  93.5 us (8%)
  starting transfers between devices  25.5 us (2%)
  between operations  23.5 us (2%)
    psum x2, blocking collectives, norm_sum(): return lax.psum(inner(rp, rc, zp, zc), ('grp', 'tile'))  205 us
    scatter-add x7, other arithmetic, segment_rows(): jax.ops.segment_sum(row, ids, num_segments=count)  171 us
    reduce_scatter x2, waiting for transfers between devices, shards(): lax.psum_scatter(segment_rows(column, owned_index, cam_grp), 'tile', scat...  161 us
    reduce_scatter x1, waiting for transfers between devices, shards(): lax.psum_scatter(group_terms, 'tile', scatter_dimension=1, tiled=True)  120 us
    all_gather x2, blocking collectives, shards(): group_cams = lax.all_gather(camera_dir, 'tile', axis=1, tiled=True)  111 us
    psum x1, blocking collectives, shards(): lax.psum(inner(point_dir, camera_dir, point_q, camera_q), ('grp', 'tile'))  106 us
    gather x4, local copies, waits for them, and re-layouts, shards(): point_term = jnp.sum(jp * point_dir[:, point_index][None], axis=1)  34.3 us
    gather x2, local copies, waits for them, and re-layouts, shards(): fetched = group_cams[:, owned_index]  30.6 us
  transfers between devices with their start and end apart: 8, of which 6 were waited for; matrix products, arithmetic and copies ran while one was open for 14% of the time, Pallas kernels for 0%

commit v1 on v0

--- a/solution.py
+++ b/solution.py
@@ -37,7 +37,7 @@
         return jnp.sum(ap * bp) + jnp.sum(ac * bc)
 
     def norm_sum(rp, rc, zp, zc):
-        return lax.psum(inner(rp, rc, zp, zc), ("grp", "tile"))
+        return lax.psum(lax.psum(inner(rp, rc, zp, zc), "grp"), "tile")
 
     point_pre = point_diag + damping
     camera_pre = camera_diag + damping

time: 1100 us -> 1160 us (1.055)
  blocking collectives: 451 us -> 519 us
    psum x1 -> x2, blocking collectives: 106 us -> 205 us  [shards(): lax.psum(inner(point_dir, camera_dir, point_q, camera_q), ('grp', 'tile'))]
    psum x2 -> x4, blocking collectives: 205 us -> 175 us  [norm_sum(): return lax.psum(lax.psum(inner(rp, rc, zp, zc), 'grp'), 'tile')]
  transfers between devices with their start and end apart: 8 -> 8, of which waited for: 6 -> 6; matrix products, arithmetic and copies ran while one was open for 14% -> 13% of each run, Pallas kernels for 0% -> 0%
where the time goes in v1:
time: 1160 us
  blocking collectives  519 us (45%)
  waiting for transfers between devices  299 us (26%)
  other arithmetic  201 us (17%)
  local copies, waits for them, and re-layouts  93.5 us (8%)
  starting transfers between devices  25.5 us (2%)
  between operations  23.5 us (2%)
    psum x2, blocking collectives, shards(): lax.psum(inner(point_dir, camera_dir, point_q, camera_q), ('grp', 'tile'))  205 us
    psum x4, blocking collectives, norm_sum(): return lax.psum(lax.psum(inner(rp, rc, zp, zc), 'grp'), 'tile')  175 us
    scatter-add x7, other arithmetic, segment_rows(): jax.ops.segment_sum(row, ids, num_segments=count)  171 us
    reduce_scatter x2, waiting for transfers between devices, shards(): lax.psum_scatter(segment_rows(column, owned_index, cam_grp), 'tile', scat...  160 us
    reduce_scatter x1, waiting for transfers between devices, shards(): lax.psum_scatter(group_terms, 'tile', scatter_dimension=1, tiled=True)  120 us
    all_gather x2, blocking collectives, shards(): group_cams = lax.all_gather(camera_dir, 'tile', axis=1, tiled=True)  112 us
    gather x4, local copies, waits for them, and re-layouts, shards(): point_term = jnp.sum(jp * point_dir[:, point_index][None], axis=1)  34.3 us
    gather x2, local copies, waits for them, and re-layouts, shards(): fetched = group_cams[:, owned_index]  30.6 us
  transfers between devices with their start and end apart: 8, of which 6 were waited for; matrix products, arithmetic and copies ran while one was open for 13% of the time, Pallas kernels for 0%

profile of v1, /device:TPU:1, one launch (start us, length us, event | category | flops | bytes accessed | tf_op | source)
XLA Modules:
  0.0 1162.2 jit_solution(4338356085256454863)
XLA Ops:
  10.1 7.6 all-to-all-start.1
  18.5 6.8 all-to-all-done.1
  29.3 7.1 all-to-all-done.2
  40.9 5.3 all-to-all-done
  46.3 25.4 %scatter_custom_fusion.2 = f32[18,12288]{0,1:T(8,128)} fusion(s32[4096]{0:T(1024)S(1)} %bitcast.80, f32[4096,18]{1,0:T(8,128)S(1)} %copy.50, f32[]{:T(128)} %constant.5.clone.1), kind=kCustom, calls=%fused_computation.15 | custom fusion | flops 73728 | bytes 884740 | tf_op jit(solution)/shard_map/vmap()/scatter-add | solution.py:13
  71.7 119.8 %reduce-scatter.4.cloned.1.call-done = f32[18,384]{0,1:T(8,128)} async-done(((f32[18,12288]{0,1:T(8,128)}), f32[18,384]{0,1:T(8,128)}) %reduce-scatter.4.cloned.1.call-update) | async-done | bytes 27664 | tf_op jit(solution)/shard_map/reduce_scatter | solution.py:33
  192.7 57.6 %all_gather.6 = f32[9,12288]{0,1:T(8,128)} all-gather(f32[9,384]{0,1:T(8,128)S(1)} %fusion.11), channel_id=1, replica_groups=mesh['grp'=16,'tile'=32] {'tile'}, dimensions={1}, use_global_device_ids=true | all-gather | bytes 456192 | tf_op jit(solution)/shard_map/all_gather | solution.py:51
  250.3 13.6 %gather_fusion.1 = f32[4096,9]{1,0:T(8,128)S(1)} fusion(f32[9,12288]{0,1:T(8,128)} %all_gather.6, s32[4096]{0:T(1024)S(1)} %broadcast_clamp_fusion), kind=kCustom, calls=%fused_computation.1 | custom fusion | bytes 311296 | tf_op jit(solution)/shard_map/gather | solution.py:52
  265.2 6.4 all-to-all-start.3
  272.3 23.8 %scatter_custom_fusion = f32[3,4096]{0,1:T(8,128)} fusion(s32[4096]{0:T(1024)S(1)} %copy-done.5, f32[4096,3]{1,0:T(8,128)S(1)} %copy.43, f32[]{:T(128)} %constant.5.clone.1), kind=kCustom, calls=%fused_computation.27 | custom fusion | flops 12288 | bytes 49156 | tf_op jit(solution)/shard_map/vmap()/scatter-add | solution.py:13
  296.8 23.7 %scatter_custom_fusion.1 = f32[3,4096]{0,1:T(8,128)} fusion(s32[4096]{0:T(1024)S(1)} %copy-done.5, f32[4096,3]{1,0:T(8,128)S(1)} %copy.44, f32[]{:T(128)} %constant.6.clone.1), kind=kCustom, calls=%fused_computation.25 | custom fusion | flops 12288 | bytes 49156 | tf_op jit(solution)/shard_map/vmap()/scatter-add | solution.py:13
  323.0 14.2 %gather_fusion = f32[4096,3]{1,0:T(8,128)} fusion(f32[3,4096]{0,1:T(8,128)S(1)} %div.21, s32[4096]{0:T(1024)S(1)} %fusion.12), kind=kCustom, calls=%fused_computation | custom fusion | bytes 114688 | tf_op jit(solution)/shard_map/gather | solution.py:53
  340.3 14.0 %all_to_all.72 = f32[9,16,256]{2,0,1:T(8,128)S(1)} all-to-all(f32[9,16,256]{2,0,1:T(8,128)S(1)} %copy.55), channel_id=1, replica_groups=mesh['grp'=16,'tile'=32] {'grp'}, dimensions={1} | all-to-all | bytes 294912 | tf_op jit(solution)/shard_map/all_to_all | solution.py:56
  356.5 25.7 %scatter_custom_fusion.4 = f32[9,12288]{0,1:T(8,128)} fusion(s32[4096]{0:T(1024)S(1)} %bitcast.82, f32[4096,9]{1,0:T(8,128)} %copy.57, f32[]{:T(128)} %constant.5.clone.1), kind=kCustom, calls=%fused_computation.13 | custom fusion | flops 36864 | bytes 442880 | tf_op jit(solution)/shard_map/vmap()/scatter-add | solution.py:13
  384.3 23.4 %scatter_fusion = f32[3,4096]{0,1:T(8,128)S(1)} fusion(f32[3,4096]{0,1:T(8,128)S(1)} %copy-done.2, s32[4096]{0:T(1024)S(1)} %copy-done.5, f32[4096,3]{1,0:T(8,128)} %copy.54), kind=kCustom, calls=%fused_computation.7 | custom fusion | flops 12288 | bytes 163840 | tf_op jit(solution)/shard_map/vmap()/scatter-add | solution.py:13
  411.2 82.1 %reduce-scatter.6.cloned.1.call-done = f32[9,384]{0,1:T(8,128)} async-done(((f32[9,12288]{0,1:T(8,128)}), f32[9,384]{0,1:T(8,128)}) %reduce-scatter.6.cloned.1.call-update) | async-done | bytes 13840 | tf_op jit(solution)/shard_map/reduce_scatter | solution.py:59
  496.3 33.9 %psum.42 = f32[]{:T(128)} all-reduce(f32[]{:T(128)S(6)} %add.107), channel_id=1, replica_groups=mesh['grp'=16,'tile'=32] {'grp'}, use_global_device_ids=true, to_apply=%region_10.0 | all-reduce | flops 1 | bytes 8 | tf_op jit(solution)/shard_map/psum | solution.py:40
  531.5 56.4 %psum.43 = f32[]{:T(128)} all-reduce(f32[]{:T(128)} %psum.42), channel_id=1, replica_groups=mesh['grp'=16,'tile'=32] {'tile'}, use_global_device_ids=true, to_apply=%region_11.0 | all-reduce | flops 1 | bytes 8 | tf_op jit(solution)/shard_map/psum | solution.py:40
  587.9 98.8 %psum.44 = f32[]{:T(128)} all-reduce(f32[]{:T(128)S(6)} %add.112), channel_id=1, replica_groups=mesh['grp'=16,'tile'=32] {'grp','tile'}, use_global_device_ids=true, to_apply=%region_21.0 | all-reduce | flops 1 | bytes 8 | tf_op jit(solution)/shard_map/psum | solution.py:65
  688.1 5.3 multiply_reduce_fusion.1
  695.4 30.3 %psum.45 = f32[]{:T(128)} all-reduce(f32[]{:T(128)S(6)} %add.113), channel_id=1, replica_groups=mesh['grp'=16,'tile'=32] {'grp'}, use_global_device_ids=true, to_apply=%region_24.0 | all-reduce | flops 1 | bytes 8 | tf_op jit(solution)/shard_map/psum | solution.py:40
  725.7 54.0 %psum.46 = f32[]{:T(128)} all-reduce(f32[]{:T(128)} %psum.45), channel_id=1, replica_groups=mesh['grp'=16,'tile'=32] {'tile'}, use_global_device_ids=true, to_apply=%region_25.0 | all-reduce | flops 1 | bytes 8 | tf_op jit(solution)/shard_map/psum | solution.py:40
  781.1 53.9 %all_gather.7 = f32[9,12288]{0,1:T(8,128)} all-gather(f32[9,384]{0,1:T(8,128)S(1)} %multiply_add_fusion.3), channel_id=1, replica_groups=mesh['grp'=16,'tile'=32] {'tile'}, dimensions={1}, use_global_device_ids=true | all-gather | bytes 456192 | tf_op jit(solution)/shard_map/all_gather | solution.py:51
  835.0 17.0 %gather_fusion.3 = f32[4096,9]{1,0:T(8,128)} fusion(f32[9,12288]{0,1:T(8,128)} %all_gather.7, s32[4096]{0:T(1024)S(1)} %broadcast_clamp_fusion), kind=kCustom, calls=%fused_computation.3 | custom fusion | bytes 311296 | tf_op jit(solution)/shard_map/gather | solution.py:52
  854.9 4.2 all-to-all-start.5
  862.6 15.7 %gather_fusion.2 = f32[4096,3]{1,0:T(8,128)} fusion(f32[3,4096]{0,1:T(8,128)} %multiply_add_fusion.1, s32[4096]{0:T(1024)S(1)} %fusion.12), kind=kCustom, calls=%fused_computation.2 | custom fusion | bytes 114688 | tf_op jit(solution)/shard_map/gather | solution.py:53
  882.2 14.4 %all_to_all.73 = f32[9,16,256]{2,0,1:T(8,128)S(1)} all-to-all(f32[9,16,256]{2,0,1:T(8,128)S(1)} %copy.62), channel_id=1, replica_groups=mesh['grp'=16,'tile'=32] {'grp'}, dimensions={1} | all-to-all | bytes 294912 | tf_op jit(solution)/shard_map/all_to_all | solution.py:56
  898.9 25.7 %scatter_custom_fusion.6 = f32[9,12288]{0,1:T(8,128)} fusion(s32[4096]{0:T(1024)S(1)} %bitcast.83, f32[4096,9]{1,0:T(8,128)} %copy.64, f32[]{:T(128)} %constant.5.clone.1), kind=kCustom, calls=%fused_computation.11 | custom fusion | flops 36864 | bytes 442880 | tf_op jit(solution)/shard_map/vmap()/scatter-add | solution.py:13
  929.6 23.3 %scatter_fusion.1 = f32[3,4096]{0,1:T(8,128)} fusion(f32[3,4096]{0,1:T(8,128)} %copy.80, s32[4096]{0:T(1024)S(1)} %copy-done.5, f32[4096,3]{1,0:T(8,128)} %copy.61), kind=kCustom, calls=%fused_computation.9 | custom fusion | flops 12288 | bytes 163840 | tf_op jit(solution)/shard_map/vmap()/scatter-add | solution.py:13
  956.3 78.0 %reduce-scatter.8.cloned.1.call-done = f32[9,384]{0,1:T(8,128)} async-done(((f32[9,12288]{0,1:T(8,128)}), f32[9,384]{0,1:T(8,128)}) %reduce-scatter.8.cloned.1.call-update) | async-done | bytes 13840 | tf_op jit(solution)/shard_map/reduce_scatter | solution.py:59
  1037.2 106.1 %psum.47 = f32[]{:T(128)} all-reduce(f32[]{:T(128)S(6)} %add.118), channel_id=1, replica_groups=mesh['grp'=16,'tile'=32] {'grp','tile'}, use_global_device_ids=true, to_apply=%region_35.0 | all-reduce | flops 1 | bytes 8 | tf_op jit(solution)/shard_map/psum | solution.py:65
  1146.2 5.3 multiply_subtract_fusion
  (102 shorter events, 60.2 us)
Async XLA Ops:
  9.1 19.8 %copy-start.7 = (f32[6,4096]{1,0:T(8,128)S(1)}, f32[6,4096]{1,0:T(8,128)}, u32[]{:S(2)}) copy-start(f32[6,4096]{1,0:T(8,128)} %param.5) | copy-start | bytes 294916
  9.1 19.8 %copy-start.6 = (f32[2,4096]{1,0:T(2,128)S(1)}, f32[2,4096]{1,0:T(2,128)}, u32[]{:S(2)}) copy-start(f32[2,4096]{1,0:T(2,128)} %param.7) | copy-start | bytes 98308
  10.1 15.3 %all-to-all-start.1 = ((f32[9,16,256]{2,0,1:T(8,128)}), f32[9,16,256]{2,0,1:T(8,128)S(1)}, u32[]{:S(2)}, u32[]{:S(2)}) async-start(f32[9,16,256]{2,0,1:T(8,128)} %copy.46), calls=%async_computation.1 | async-start | bytes 524288 | tf_op jit(solution)/shard_map/all_to_all | solution.py:25
  25.3 11.0 all-to-all-start.2
  36.4 9.9 all-to-all-start
  39.9 151.6 %reduce-scatter.4.cloned.1.call-start = ((), (), s32[]{:S(2)}) async-start(), calls=%async_computation.10 | async-start | bytes 6488064 | tf_op jit(solution)/shard_map/reduce_scatter | solution.py:33
  250.2 21.4 %copy-start.5 = (s32[4096]{0:T(1024)S(1)}, s32[4096]{0:T(1024)}, u32[]{:S(2)}) copy-start(s32[4096]{0:T(1024)} %param.8) | copy-start | bytes 49156
  265.2 74.4 %all-to-all-start.3 = ((f32[9,16,256]{2,0,1:T(8,128)}), f32[9,16,256]{2,0,1:T(8,128)S(1)}, u32[]{:S(2)}, u32[]{:S(2)}) async-start(f32[9,16,256]{2,0,1:T(8,128)} %copy.52), calls=%async_computation.4 | async-start | bytes 524288 | tf_op jit(solution)/shard_map/all_to_all | solution.py:54
  271.6 221.7 %reduce-scatter.6.cloned.1.call-start = ((), (), s32[]{:S(2)}) async-start(), calls=%async_computation.11 | async-start | bytes 6488064 | tf_op jit(solution)/shard_map/reduce_scatter | solution.py:59
  323.0 59.2 %copy-start = (f32[3,4096]{0,1:T(8,128)}, f32[3,4096]{0,1:T(8,128)S(1)}, u32[]{:S(2)}) copy-start(f32[3,4096]{0,1:T(8,128)S(1)} %div.21) | copy-start | bytes 147460
  382.3 2.1 copy-start.2
  407.8 85.6 %copy-start.3 = (f32[18,384]{0,1:T(8,128)S(1)}, f32[18,384]{0,1:T(8,128)}, u32[]{:S(2)}) copy-start(f32[18,384]{0,1:T(8,128)} %reduce-scatter.4.cloned.1.call-done) | copy-start | bytes 82948
  835.0 24.4 %copy-start.1 = (f32[3,4096]{0,1:T(8,128)S(1)}, f32[3,4096]{0,1:T(8,128)}, u32[]{:S(2)}) copy-start(f32[3,4096]{0,1:T(8,128)} %copy-done) | copy-start | bytes 147460
  854.9 25.6 %all-to-all-start.5 = ((f32[9,16,256]{2,0,1:T(8,128)}), f32[9,16,256]{2,0,1:T(8,128)}, u32[]{:S(2)}, u32[]{:S(2)}) async-start(f32[9,16,256]{2,0,1:T(8,128)} %copy.59), calls=%async_computation.7 | async-start | bytes 524288 | tf_op jit(solution)/shard_map/all_to_all | solution.py:54
  859.1 175.1 %reduce-scatter.8.cloned.1.call-start = ((), (), s32[]{:S(2)}) async-start(), calls=%async_computation.12 | async-start | bytes 6488064 | tf_op jit(solution)/shard_map/reduce_scatter | solution.py:59
  1151.5 3.0 copy-start.4
Sparse Core Ops, SparseCore 0:
  71.8 119.6 reduce-scatter.3
  382.4 110.9 reduce-scatter.5
  924.7 109.5 reduce-scatter.7
